TPU v7x, 256 devices: a whole 4x4x8 slice. The times are simulated.
256 devices in a mesh: dom: 64 (over x, z, core), slab: 4 (over y).
Axes of the slice: x: 4, y: 4, z: 8, core: 2. Of those that a mesh axis runs over, the one named last changes fastest.
Arguments:
- logperm: float32 [256, 16, 64, 128], P('dom', 'slab'), may hold values from -4.2 to 4.2
- source: float32 [16, 64, 128], P('slab'), may hold values from -6 to 6
- observed: float32 [16, 64, 128], P('slab'), may hold values from -1.2 to 1.2
- brownian: float32 [256, 256], replicated, may hold values from -6 to 6
Outputs:
- particles_next: float32 [256, 16, 64, 128], P('dom', 'slab')
All inputs are finite; a program needn't handle non-finite values.
Results may differ from a plain program's by a relative error of at most 0.0003.
Values sent between devices are 32-bit elements; how exact they have to be, the bound alone decides.
No kernel may reach another device: no remote copies, remote signals or barrier semaphores. Data moves between devices by JAX's collectives and lax.ppermute only.
A program may use at most 64 MiB of HBM per device.

v0:
```python
import math
import jax
import jax.numpy as jnp
from jax import lax
from jax.sharding import PartitionSpec as P

SWEEPS = 8
misfit_weight = 1000.0


def with_halo(block, sides, width):
    for axis, dim in sides:
        count = lax.axis_size(axis)
        forward = [(i, i + 1) for i in range(count - 1)]
        backward = [(target, source) for source, target in forward]
        low = lax.ppermute(
            lax.slice_in_dim(block, block.shape[dim] - width, None, axis=dim), axis, forward
        )
        high = lax.ppermute(lax.slice_in_dim(block, 0, width, axis=dim), axis, backward)
        block = jnp.concatenate([low, block, high], axis=dim)
    return block


def neighbor_sum(core, below, above, fill):
    pad_y = jnp.pad(core, ((0, 0), (0, 0), (1, 1), (0, 0)), constant_values=fill)
    pad_z = jnp.pad(core, ((0, 0), (0, 0), (0, 0), (1, 1)), constant_values=fill)
    return below + above + pad_y[:, :, :-2] + pad_y[:, :, 2:] + pad_z[..., :-2] + pad_z[..., 2:]


def grad_field(e_core, e_below, e_above, p_core, p_below, p_above, q_core, q_below, q_above):
    summed = e_below * (p_core - p_below) * (q_core - q_below) + e_above * (p_core - p_above) * (
        q_core - q_above
    )
    for dimension in (2, 3):
        padding = [(0, 0), (0, 0), (0, 0), (0, 0)]
        padding[dimension] = (1, 1)
        e_pad = jnp.pad(e_core, padding, constant_values=1.0)
        p_pad = jnp.pad(p_core, padding)
        q_pad = jnp.pad(q_core, padding)
        extent = e_core.shape[dimension]
        for offset in (0, 2):
            e_near = lax.slice_in_dim(e_pad, offset, offset + extent, axis=dimension)
            p_near = lax.slice_in_dim(p_pad, offset, offset + extent, axis=dimension)
            q_near = lax.slice_in_dim(q_pad, offset, offset + extent, axis=dimension)
            summed = summed + e_near * (p_core - p_near) * (q_core - q_near)
    return -0.5 * e_core * summed


def on_device(logperm, source, observed, brownian):
    particles, width, rows_y, depth_z = logperm.shape
    slabs = lax.axis_size("slab")
    cells = width * slabs * rows_y * depth_z
    extended = with_halo(logperm, (("slab", 1),), 1)
    e_ext = jnp.exp(0.5 * extended)
    e_core = e_ext[:, 1:-1]
    inverse = 1.0 / neighbor_sum(e_core, e_ext[:, :-2], e_ext[:, 2:], 1.0)

    def relax_rim(rhs):
        value = inverse * rhs
        for sweep_index in range(SWEEPS - 1):
            bordered = with_halo(value, (("slab", 1),), 1)
            value = inverse * (
                rhs + e_core * neighbor_sum(value, bordered[:, :-2], bordered[:, 2:], 0.0)
            )
        return value / e_core

    pressure = relax_rim(source[None])
    misfit = misfit_weight * (pressure - observed[None])
    adjoint = relax_rim(misfit)
    states = with_halo(jnp.stack([pressure, adjoint]), (("slab", 2),), 1)
    gradient = grad_field(
        e_core,
        e_ext[:, :-2],
        e_ext[:, 2:],
        pressure,
        states[0][:, :-2],
        states[0][:, 2:],
        adjoint,
        states[1][:, :-2],
        states[1][:, 2:],
    )
    g_flat = gradient.reshape(particles, -1)
    u_cells, g_cells = (
        lax.all_to_all(
            logperm.reshape(particles, -1), "dom", split_axis=1, concat_axis=0, tiled=True
        ),
        lax.all_to_all(g_flat, "dom", split_axis=1, concat_axis=0, tiled=True),
    )
    ensemble = u_cells.shape[0]
    centre = jnp.mean(u_cells, axis=0, keepdims=True)
    spread = u_cells - centre
    partial_gram = lax.dot_general(
        spread,
        g_cells,
        (((1,), (1,)), ((), ())),
        precision=lax.Precision.HIGHEST,
        preferred_element_type=jnp.float32,
    )
    gram = lax.psum(partial_gram, ("dom", "slab"))
    step_size = ensemble / (4.0 * (cells + 1))
    mixing = -(step_size / ensemble) * gram + math.sqrt(2.0 * step_size / ensemble) * brownian
    moved = (
        centre
        + 1.25 * spread
        + lax.dot_general(
            mixing,
            spread,
            (((0,), (0,)), ((), ())),
            precision=lax.Precision.HIGHEST,
            preferred_element_type=jnp.float32,
        )
    )
    returned = lax.all_to_all(moved, "dom", split_axis=0, concat_axis=1, tiled=True)
    return returned.reshape(logperm.shape)


def solution(mesh):
    return jax.shard_map(
        on_device,
        mesh=mesh,
        in_specs=(P("dom", "slab", None, None), P("slab", None, None), P("slab", None, None), P()),
        out_specs=P("dom", "slab", None, None),
        check_vma=False,
    )
```

profile of v0, /device:TPU:1, one launch (start us, length us, event | category | flops | bytes accessed | tf_op | source)
XLA Modules:
  0.0 498.0 jit_solution(12891519340523834035)
XLA Ops:
  7.6 4.0 collective-permute-start
  13.7 3.6 collective-permute-done.1
  18.9 3.2 collective-permute-start.2
  24.1 3.8 collective-permute-done.3
  28.3 2.9 collective-permute-start.4
  33.1 3.8 collective-permute-done.5
  41.5 3.8 collective-permute-done.7
  49.5 3.8 collective-permute-done.9
  57.6 3.8 collective-permute-done.11
  66.1 4.1 collective-permute-done.13
  75.3 3.9 collective-permute-done.15
  84.2 3.8 collective-permute-done.17
  92.6 3.8 collective-permute-done.19
  101.0 3.8 collective-permute-done.21
  109.4 3.8 collective-permute-done.23
  117.5 3.8 collective-permute-done.25
  125.7 3.8 collective-permute-done.27
  133.8 3.9 collective-permute-done.29
  144.2 28.9 %all-to-all-start = ((f32[4,64,512]{2,0,1:T(4,128)}), f32[4,64,512]{2,0,1:T(4,128)S(1)}, u32[]{:S(2)}, u32[]{:S(2)}) async-start(f32[4,64,512]{2,0,1:T(4,128)} %copy.7), calls=%async_computation | async-start | bytes 1048576 | tf_op jit(solution)/shard_map/all_to_all | solution.py:84
  176.8 13.7 %all-to-all-done = f32[4,64,512]{2,0,1:T(4,128)S(1)} async-done(((f32[4,64,512]{2,0,1:T(4,128)}), f32[4,64,512]{2,0,1:T(4,128)S(1)}, u32[]{:S(2)}, u32[]{:S(2)}) %all-to-all-start) | async-done | bytes 524320 | tf_op jit(solution)/shard_map/all_to_all | solution.py:84
  190.4 6.3 %all-to-all-start.1 = ((f32[4,64,512]{2,0,1:T(4,128)}), f32[4,64,512]{2,0,1:T(4,128)S(1)}, u32[]{:S(2)}, u32[]{:S(2)}) async-start(f32[4,64,512]{2,0,1:T(4,128)} %copy.8), calls=%async_computation.1 | async-start | bytes 1048576 | tf_op jit(solution)/shard_map/all_to_all | solution.py:87
  197.2 16.9 %all-to-all-done.1 = f32[4,64,512]{2,0,1:T(4,128)S(1)} async-done(((f32[4,64,512]{2,0,1:T(4,128)}), f32[4,64,512]{2,0,1:T(4,128)S(1)}, u32[]{:S(2)}, u32[]{:S(2)}) %all-to-all-start.1) | async-done | bytes 524320 | tf_op jit(solution)/shard_map/all_to_all | solution.py:87
  215.8 245.4 %all-reduce.36.cloned.1.call-done = f32[256,256]{1,0:T(8,128)} async-done(((f32[256,256]{1,0:T(8,128)}), f32[256,256]{1,0:T(8,128)}) %all-reduce.36.cloned.1.call-update) | async-done | bytes 262160 | tf_op jit(solution)/shard_map/psum | solution.py:99
  462.9 27.3 %all_to_all.54 = f32[64,4,512]{2,1,0:T(4,128)S(1)} all-to-all(f32[64,4,512]{2,1,0:T(4,128)S(1)} %all_to_all.48), channel_id=1, replica_groups=mesh['dom'=64,'slab'=4] {'dom'}, dimensions={0} | all-to-all | bytes 1048576 | tf_op jit(solution)/shard_map/all_to_all | solution.py:113
  (107 shorter events, 78.3 us)
Async XLA Ops:
  7.6 6.2 %collective-permute-start = (f32[4,1,64,128]{3,2,1,0:T(8,128)S(1)}, f32[4,1,64,128]{3,2,1,0:T(8,128)S(1)}, u32[]{:S(2)}, u32[]{:S(2)}) collective-permute-start(f32[4,1,64,128]{3,2,1,0:T(8,128)S(1)} %get-tuple-element.41), channel_id=1, source_target_pairs={{0,1},{1,2},{2,3},{4,5},{5,6},{6,7},{8,9},{9,10},{10,11},{12,13},{... | collective-permute-start | bytes 393224 | tf_op jit(solution)/shard_map/ppermute | solution.py:16
  11.6 5.7 %collective-permute-start.1 = (f32[4,1,64,128]{3,2,1,0:T(8,128)S(1)}, f32[4,1,64,128]{3,2,1,0:T(8,128)S(1)}, u32[]{:S(2)}, u32[]{:S(2)}) collective-permute-start(f32[4,1,64,128]{3,2,1,0:T(8,128)S(1)} %get-tuple-element.42), channel_id=1, source_target_pairs={{1,0},{2,1},{3,2},{5,4},{6,5},{7,6},{9,8},{10,9},{11,10},{13,12},{... | collective-permute-start | bytes 393224 | tf_op jit(solution)/shard_map/ppermute | solution.py:19
  18.9 5.1 %collective-permute-start.2 = (f32[4,1,64,128]{3,2,1,0:T(8,128)S(1)}, f32[4,1,64,128]{3,2,1,0:T(8,128)S(1)}, u32[]{:S(2)}, u32[]{:S(2)}) collective-permute-start(f32[4,1,64,128]{3,2,1,0:T(8,128)S(1)} %get-tuple-element.39), channel_id=1, source_target_pairs={{0,1},{1,2},{2,3},{4,5},{5,6},{6,7},{8,9},{9,10},{10,11},{12,13},{... | collective-permute-start | bytes 393224 | tf_op jit(solution)/shard_map/ppermute | solution.py:16
  22.2 5.7 %collective-permute-start.3 = (f32[4,1,64,128]{3,2,1,0:T(8,128)S(1)}, f32[4,1,64,128]{3,2,1,0:T(8,128)S(1)}, u32[]{:S(2)}, u32[]{:S(2)}) collective-permute-start(f32[4,1,64,128]{3,2,1,0:T(8,128)S(1)} %get-tuple-element.40), channel_id=1, source_target_pairs={{1,0},{2,1},{3,2},{5,4},{6,5},{7,6},{9,8},{10,9},{11,10},{13,12},{... | collective-permute-start | bytes 393224 | tf_op jit(solution)/shard_map/ppermute | solution.py:19
  28.3 4.8 collective-permute-start.4
  31.2 5.7 %collective-permute-start.5 = (f32[4,1,64,128]{3,2,1,0:T(8,128)S(1)}, f32[4,1,64,128]{3,2,1,0:T(8,128)S(1)}, u32[]{:S(2)}, u32[]{:S(2)}) collective-permute-start(f32[4,1,64,128]{3,2,1,0:T(8,128)S(1)} %get-tuple-element.38), channel_id=1, source_target_pairs={{1,0},{2,1},{3,2},{5,4},{6,5},{7,6},{9,8},{10,9},{11,10},{13,12},{... | collective-permute-start | bytes 393224 | tf_op jit(solution)/shard_map/ppermute | solution.py:19
  39.6 5.7 %collective-permute-start.7 = (f32[4,1,64,128]{3,2,1,0:T(8,128)S(1)}, f32[4,1,64,128]{3,2,1,0:T(8,128)S(1)}, u32[]{:S(2)}, u32[]{:S(2)}) collective-permute-start(f32[4,1,64,128]{3,2,1,0:T(8,128)S(1)} %get-tuple-element.36), channel_id=1, source_target_pairs={{1,0},{2,1},{3,2},{5,4},{6,5},{7,6},{9,8},{10,9},{11,10},{13,12},{... | collective-permute-start | bytes 393224 | tf_op jit(solution)/shard_map/ppermute | solution.py:19
  47.6 5.7 %collective-permute-start.9 = (f32[4,1,64,128]{3,2,1,0:T(8,128)S(1)}, f32[4,1,64,128]{3,2,1,0:T(8,128)S(1)}, u32[]{:S(2)}, u32[]{:S(2)}) collective-permute-start(f32[4,1,64,128]{3,2,1,0:T(8,128)S(1)} %get-tuple-element.34), channel_id=1, source_target_pairs={{1,0},{2,1},{3,2},{5,4},{6,5},{7,6},{9,8},{10,9},{11,10},{13,12},{... | collective-permute-start | bytes 393224 | tf_op jit(solution)/shard_map/ppermute | solution.py:19
  55.7 5.7 %collective-permute-start.11 = (f32[4,1,64,128]{3,2,1,0:T(8,128)S(1)}, f32[4,1,64,128]{3,2,1,0:T(8,128)S(1)}, u32[]{:S(2)}, u32[]{:S(2)}) collective-permute-start(f32[4,1,64,128]{3,2,1,0:T(8,128)S(1)} %get-tuple-element.32), channel_id=1, source_target_pairs={{1,0},{2,1},{3,2},{5,4},{6,5},{7,6},{9,8},{10,9},{11,10},{13,12},{... | collective-permute-start | bytes 393224 | tf_op jit(solution)/shard_map/ppermute | solution.py:19
  63.9 6.3 %collective-permute-start.13 = (f32[4,1,64,128]{3,2,1,0:T(8,128)S(1)}, f32[4,1,64,128]{3,2,1,0:T(8,128)S(1)}, u32[]{:S(2)}, u32[]{:S(2)}) collective-permute-start(f32[4,1,64,128]{3,2,1,0:T(8,128)S(1)} %get-tuple-element.30), channel_id=1, source_target_pairs={{1,0},{2,1},{3,2},{5,4},{6,5},{7,6},{9,8},{10,9},{11,10},{13,12},{... | collective-permute-start | bytes 393224 | tf_op jit(solution)/shard_map/ppermute | solution.py:19
  70.6 4.7 collective-permute-start.14
  72.3 7.0 %collective-permute-start.15 = (f32[4,1,64,128]{3,2,1,0:T(8,128)S(1)}, f32[4,1,64,128]{3,2,1,0:T(8,128)S(1)}, u32[]{:S(2)}, u32[]{:S(2)}) collective-permute-start(f32[4,1,64,128]{3,2,1,0:T(8,128)S(1)} %get-tuple-element.28), channel_id=1, source_target_pairs={{1,0},{2,1},{3,2},{5,4},{6,5},{7,6},{9,8},{10,9},{11,10},{13,12},{... | collective-permute-start | bytes 393224 | tf_op jit(solution)/shard_map/ppermute | solution.py:19
  81.9 6.1 %collective-permute-start.17 = (f32[4,1,64,128]{3,2,1,0:T(8,128)S(1)}, f32[4,1,64,128]{3,2,1,0:T(8,128)S(1)}, u32[]{:S(2)}, u32[]{:S(2)}) collective-permute-start(f32[4,1,64,128]{3,2,1,0:T(8,128)S(1)} %get-tuple-element.26), channel_id=1, source_target_pairs={{1,0},{2,1},{3,2},{5,4},{6,5},{7,6},{9,8},{10,9},{11,10},{13,12},{... | collective-permute-start | bytes 393224 | tf_op jit(solution)/shard_map/ppermute | solution.py:19
  90.7 5.7 %collective-permute-start.19 = (f32[4,1,64,128]{3,2,1,0:T(8,128)S(1)}, f32[4,1,64,128]{3,2,1,0:T(8,128)S(1)}, u32[]{:S(2)}, u32[]{:S(2)}) collective-permute-start(f32[4,1,64,128]{3,2,1,0:T(8,128)S(1)} %get-tuple-element.24), channel_id=1, source_target_pairs={{1,0},{2,1},{3,2},{5,4},{6,5},{7,6},{9,8},{10,9},{11,10},{13,12},{... | collective-permute-start | bytes 393224 | tf_op jit(solution)/shard_map/ppermute | solution.py:19
  99.1 5.7 %collective-permute-start.21 = (f32[4,1,64,128]{3,2,1,0:T(8,128)S(1)}, f32[4,1,64,128]{3,2,1,0:T(8,128)S(1)}, u32[]{:S(2)}, u32[]{:S(2)}) collective-permute-start(f32[4,1,64,128]{3,2,1,0:T(8,128)S(1)} %get-tuple-element.22), channel_id=1, source_target_pairs={{1,0},{2,1},{3,2},{5,4},{6,5},{7,6},{9,8},{10,9},{11,10},{13,12},{... | collective-permute-start | bytes 393224 | tf_op jit(solution)/shard_map/ppermute | solution.py:19
  107.5 5.7 %collective-permute-start.23 = (f32[4,1,64,128]{3,2,1,0:T(8,128)S(1)}, f32[4,1,64,128]{3,2,1,0:T(8,128)S(1)}, u32[]{:S(2)}, u32[]{:S(2)}) collective-permute-start(f32[4,1,64,128]{3,2,1,0:T(8,128)S(1)} %get-tuple-element.20), channel_id=1, source_target_pairs={{1,0},{2,1},{3,2},{5,4},{6,5},{7,6},{9,8},{10,9},{11,10},{13,12},{... | collective-permute-start | bytes 393224 | tf_op jit(solution)/shard_map/ppermute | solution.py:19
  115.6 5.7 %collective-permute-start.25 = (f32[4,1,64,128]{3,2,1,0:T(8,128)S(1)}, f32[4,1,64,128]{3,2,1,0:T(8,128)S(1)}, u32[]{:S(2)}, u32[]{:S(2)}) collective-permute-start(f32[4,1,64,128]{3,2,1,0:T(8,128)S(1)} %get-tuple-element.18), channel_id=1, source_target_pairs={{1,0},{2,1},{3,2},{5,4},{6,5},{7,6},{9,8},{10,9},{11,10},{13,12},{... | collective-permute-start | bytes 393224 | tf_op jit(solution)/shard_map/ppermute | solution.py:19
  123.8 5.7 %collective-permute-start.27 = (f32[4,1,64,128]{3,2,1,0:T(8,128)S(1)}, f32[4,1,64,128]{3,2,1,0:T(8,128)S(1)}, u32[]{:S(2)}, u32[]{:S(2)}) collective-permute-start(f32[4,1,64,128]{3,2,1,0:T(8,128)S(1)} %get-tuple-element.16), channel_id=1, source_target_pairs={{1,0},{2,1},{3,2},{5,4},{6,5},{7,6},{9,8},{10,9},{11,10},{13,12},{... | collective-permute-start | bytes 393224 | tf_op jit(solution)/shard_map/ppermute | solution.py:19
  131.9 5.8 %collective-permute-start.29 = (f32[4,1,64,128]{3,2,1,0:T(8,128)S(1)}, f32[4,1,64,128]{3,2,1,0:T(8,128)S(1)}, u32[]{:S(2)}, u32[]{:S(2)}) collective-permute-start(f32[4,1,64,128]{3,2,1,0:T(8,128)S(1)} %get-tuple-element.14), channel_id=1, source_target_pairs={{1,0},{2,1},{3,2},{5,4},{6,5},{7,6},{9,8},{10,9},{11,10},{13,12},{... | collective-permute-start | bytes 393224 | tf_op jit(solution)/shard_map/ppermute | solution.py:19
  139.1 34.0 %collective-permute-start.30 = (f32[2,4,1,64,128]{4,3,2,1,0:T(8,128)}, f32[2,4,1,64,128]{4,3,2,1,0:T(8,128)}, u32[]{:S(2)}, u32[]{:S(2)}) collective-permute-start(f32[2,4,1,64,128]{4,3,2,1,0:T(8,128)} %get-tuple-element.11), channel_id=1, source_target_pairs={{0,1},{1,2},{2,3},{4,5},{5,6},{6,7},{8,9},{9,10},{10,11},{12,13},{... | collective-permute-start | bytes 786440 | tf_op jit(solution)/shard_map/ppermute | solution.py:16
  141.7 31.4 %collective-permute-start.31 = (f32[2,4,1,64,128]{4,3,2,1,0:T(8,128)}, f32[2,4,1,64,128]{4,3,2,1,0:T(8,128)}, u32[]{:S(2)}, u32[]{:S(2)}) collective-permute-start(f32[2,4,1,64,128]{4,3,2,1,0:T(8,128)} %get-tuple-element.12), channel_id=1, source_target_pairs={{1,0},{2,1},{3,2},{5,4},{6,5},{7,6},{9,8},{10,9},{11,10},{13,12},{... | collective-permute-start | bytes 786440 | tf_op jit(solution)/shard_map/ppermute | solution.py:19
  144.2 46.2 %all-to-all-start = ((f32[4,64,512]{2,0,1:T(4,128)}), f32[4,64,512]{2,0,1:T(4,128)S(1)}, u32[]{:S(2)}, u32[]{:S(2)}) async-start(f32[4,64,512]{2,0,1:T(4,128)} %copy.7), calls=%async_computation | async-start | bytes 1048576 | tf_op jit(solution)/shard_map/all_to_all | solution.py:84
  190.4 23.6 %all-to-all-start.1 = ((f32[4,64,512]{2,0,1:T(4,128)}), f32[4,64,512]{2,0,1:T(4,128)S(1)}, u32[]{:S(2)}, u32[]{:S(2)}) async-start(f32[4,64,512]{2,0,1:T(4,128)} %copy.8), calls=%async_computation.1 | async-start | bytes 1048576 | tf_op jit(solution)/shard_map/all_to_all | solution.py:87
  196.7 264.4 %all-reduce.36.cloned.1.call-start = ((), (), s32[]{:S(2)}) async-start(), calls=%async_computation.3 | async-start | bytes 524288 | tf_op jit(solution)/shard_map/psum | solution.py:99
  (15 other events, 332.0 us)
Sparse Core Ops, SparseCore 0:
  215.7 245.3 all-reduce.35
where the time goes:
time: 499 us; the launch traced here: 498 us
  waiting for transfers between devices  344 us (69%)
  starting transfers between devices  93 us (19%)
  blocking collectives  27.3 us (5%)
  between operations  14.1 us (3%)
  other arithmetic  10.8 us (2%)
  local copies, waits for them, and re-layouts  5.66 us (1%)
    psum x1, waiting for transfers between devices, on_device(): gram = lax.psum(partial_gram, ('dom', 'slab'))  245 us
    ppermute x16, waiting for transfers between devices, with_halo(): lax.ppermute(lax.slice_in_dim(block, 0, width, axis=dim), axis, backward)  57.2 us
    ppermute x16, starting transfers between devices, with_halo(): lax.ppermute(lax.slice_in_dim(block, block.shape[dim] - width, None, axis...  37 us
    all_to_all x1, starting transfers between devices, on_device(): lax.all_to_all(logperm.reshape(particles, -1), 'dom', split_axis=1, conca...  28.9 us
    all_to_all x1, blocking collectives, on_device(): lax.all_to_all(moved, 'dom', split_axis=0, concat_axis=1, tiled=True)  27.3 us
    ppermute x16, starting transfers between devices, with_halo(): lax.ppermute(lax.slice_in_dim(block, 0, width, axis=dim), axis, backward)  20.8 us
    all_to_all x1, waiting for transfers between devices, on_device(): lax.all_to_all(g_flat, 'dom', split_axis=1, concat_axis=0, tiled=True)  16.9 us
    all_to_all x1, waiting for transfers between devices, on_device(): lax.all_to_all(logperm.reshape(particles, -1), 'dom', split_axis=1, conca...  13.7 us
  transfers between devices with their start and end apart: 35, of which 33 were waited for; matrix products, arithmetic and copies ran while one was open for 1% of the time, Pallas kernels for 0%

commit v1 on v0

--- a/solution.py
+++ b/solution.py
@@ -96,7 +96,7 @@
         precision=lax.Precision.HIGHEST,
         preferred_element_type=jnp.float32,
     )
-    gram = lax.psum(partial_gram, ("dom", "slab"))
+    gram = lax.psum(lax.psum(partial_gram, "dom"), "slab")
     step_size = ensemble / (4.0 * (cells + 1))
     mixing = -(step_size / ensemble) * gram + math.sqrt(2.0 * step_size / ensemble) * brownian
     moved = (

time: 499 us -> 473 us (0.948)
  waiting for transfers between devices: 344 us -> 315 us
    psum x1 -> x2, waiting for transfers between devices: 245 us -> 216 us  [on_device(): gram = lax.psum(lax.psum(partial_gram, 'dom'), 'slab')]
  transfers between devices with their start and end apart: 35 -> 36, of which waited for: 33 -> 34; matrix products, arithmetic and copies ran while one was open for 1% -> 1% of each run, Pallas kernels for 0% -> 0%
where the time goes in v1:
time: 473 us; the launch traced here: 472 us
  waiting for transfers between devices  315 us (67%)
  starting transfers between devices  93 us (20%)
  blocking collectives  29.9 us (6%)
  between operations  14.1 us (3%)
  other arithmetic  10.8 us (2%)
  local copies, waits for them, and re-layouts  5.66 us (1%)
    psum x2, waiting for transfers between devices, on_device(): gram = lax.psum(lax.psum(partial_gram, 'dom'), 'slab')  216 us
    ppermute x16, waiting for transfers between devices, with_halo(): lax.ppermute(lax.slice_in_dim(block, 0, width, axis=dim), axis, backward)  57.2 us
    ppermute x16, starting transfers between devices, with_halo(): lax.ppermute(lax.slice_in_dim(block, block.shape[dim] - width, None, axis...  37 us
    all_to_all x1, blocking collectives, on_device(): lax.all_to_all(moved, 'dom', split_axis=0, concat_axis=1, tiled=True)  29.9 us
    all_to_all x1, starting transfers between devices, on_device(): lax.all_to_all(logperm.reshape(particles, -1), 'dom', split_axis=1, conca...  28.9 us
    ppermute x16, starting transfers between devices, with_halo(): lax.ppermute(lax.slice_in_dim(block, 0, width, axis=dim), axis, backward)  20.8 us
    all_to_all x1, waiting for transfers between devices, on_device(): lax.all_to_all(g_flat, 'dom', split_axis=1, concat_axis=0, tiled=True)  16.9 us
    all_to_all x1, waiting for transfers between devices, on_device(): lax.all_to_all(logperm.reshape(particles, -1), 'dom', split_axis=1, conca...  13.7 us
  transfers between devices with their start and end apart: 36, of which 34 were waited for; matrix products, arithmetic and copies ran while one was open for 1% of the time, Pallas kernels for 0%

profile of v1, /device:TPU:1, one launch (start us, length us, event | category | flops | bytes accessed | tf_op | source)
XLA Modules:
  0.0 471.7 jit_solution(7714318694255793960)
XLA Ops:
  7.6 4.0 collective-permute-start
  13.7 3.6 collective-permute-done.1
  18.9 3.2 collective-permute-start.2
  24.1 3.8 collective-permute-done.3
  33.1 3.8 collective-permute-done.5
  41.5 3.8 collective-permute-done.7
  49.5 3.8 collective-permute-done.9
  57.6 3.8 collective-permute-done.11
  66.1 4.1 collective-permute-done.13
  75.3 3.9 collective-permute-done.15
  84.2 3.8 collective-permute-done.17
  92.6 3.8 collective-permute-done.19
  101.0 3.8 collective-permute-done.21
  109.4 3.8 collective-permute-done.23
  117.5 3.8 collective-permute-done.25
  125.7 3.8 collective-permute-done.27
  133.8 3.9 collective-permute-done.29
  144.2 28.9 %all-to-all-start = ((f32[4,64,512]{2,0,1:T(4,128)}), f32[4,64,512]{2,0,1:T(4,128)S(1)}, u32[]{:S(2)}, u32[]{:S(2)}) async-start(f32[4,64,512]{2,0,1:T(4,128)} %copy.7), calls=%async_computation | async-start | bytes 1048576 | tf_op jit(solution)/shard_map/all_to_all | solution.py:84
  176.8 13.7 %all-to-all-done = f32[4,64,512]{2,0,1:T(4,128)S(1)} async-done(((f32[4,64,512]{2,0,1:T(4,128)}), f32[4,64,512]{2,0,1:T(4,128)S(1)}, u32[]{:S(2)}, u32[]{:S(2)}) %all-to-all-start) | async-done | bytes 524320 | tf_op jit(solution)/shard_map/all_to_all | solution.py:84
  190.4 6.3 %all-to-all-start.1 = ((f32[4,64,512]{2,0,1:T(4,128)}), f32[4,64,512]{2,0,1:T(4,128)S(1)}, u32[]{:S(2)}, u32[]{:S(2)}) async-start(f32[4,64,512]{2,0,1:T(4,128)} %copy.8), calls=%async_computation.1 | async-start | bytes 1048576 | tf_op jit(solution)/shard_map/all_to_all | solution.py:87
  197.2 16.9 %all-to-all-done.1 = f32[4,64,512]{2,0,1:T(4,128)S(1)} async-done(((f32[4,64,512]{2,0,1:T(4,128)}), f32[4,64,512]{2,0,1:T(4,128)S(1)}, u32[]{:S(2)}, u32[]{:S(2)}) %all-to-all-start.1) | async-done | bytes 524320 | tf_op jit(solution)/shard_map/all_to_all | solution.py:87
  215.6 172.2 %all-reduce.37.cloned.1.call-done = f32[256,256]{1,0:T(8,128)} async-done(((f32[256,256]{1,0:T(8,128)}), f32[256,256]{1,0:T(8,128)}) %all-reduce.37.cloned.1.call-update) | async-done | bytes 262160 | tf_op jit(solution)/shard_map/psum | solution.py:99
  388.0 44.1 %all-reduce.39.cloned.1.call-done = f32[256,256]{1,0:T(8,128)} async-done(((f32[256,256]{1,0:T(8,128)}), f32[256,256]{1,0:T(8,128)}) %all-reduce.39.cloned.1.call-update) | async-done | bytes 262160 | tf_op jit(solution)/shard_map/psum | solution.py:99
  433.9 29.9 %all_to_all.54 = f32[64,4,512]{2,1,0:T(4,128)S(1)} all-to-all(f32[64,4,512]{2,1,0:T(4,128)S(1)} %all_to_all.48), channel_id=1, replica_groups=mesh['dom'=64,'slab'=4] {'dom'}, dimensions={0} | all-to-all | bytes 1048576 | tf_op jit(solution)/shard_map/all_to_all | solution.py:113
  (110 shorter events, 81.3 us)
Async XLA Ops:
  7.6 6.2 %collective-permute-start = (f32[4,1,64,128]{3,2,1,0:T(8,128)S(1)}, f32[4,1,64,128]{3,2,1,0:T(8,128)S(1)}, u32[]{:S(2)}, u32[]{:S(2)}) collective-permute-start(f32[4,1,64,128]{3,2,1,0:T(8,128)S(1)} %get-tuple-element.41), channel_id=1, source_target_pairs={{0,1},{1,2},{2,3},{4,5},{5,6},{6,7},{8,9},{9,10},{10,11},{12,13},{... | collective-permute-start | bytes 393224 | tf_op jit(solution)/shard_map/ppermute | solution.py:16
  11.6 5.7 %collective-permute-start.1 = (f32[4,1,64,128]{3,2,1,0:T(8,128)S(1)}, f32[4,1,64,128]{3,2,1,0:T(8,128)S(1)}, u32[]{:S(2)}, u32[]{:S(2)}) collective-permute-start(f32[4,1,64,128]{3,2,1,0:T(8,128)S(1)} %get-tuple-element.42), channel_id=1, source_target_pairs={{1,0},{2,1},{3,2},{5,4},{6,5},{7,6},{9,8},{10,9},{11,10},{13,12},{... | collective-permute-start | bytes 393224 | tf_op jit(solution)/shard_map/ppermute | solution.py:19
  18.9 5.1 %collective-permute-start.2 = (f32[4,1,64,128]{3,2,1,0:T(8,128)S(1)}, f32[4,1,64,128]{3,2,1,0:T(8,128)S(1)}, u32[]{:S(2)}, u32[]{:S(2)}) collective-permute-start(f32[4,1,64,128]{3,2,1,0:T(8,128)S(1)} %get-tuple-element.39), channel_id=1, source_target_pairs={{0,1},{1,2},{2,3},{4,5},{5,6},{6,7},{8,9},{9,10},{10,11},{12,13},{... | collective-permute-start | bytes 393224 | tf_op jit(solution)/shard_map/ppermute | solution.py:16
  22.2 5.7 %collective-permute-start.3 = (f32[4,1,64,128]{3,2,1,0:T(8,128)S(1)}, f32[4,1,64,128]{3,2,1,0:T(8,128)S(1)}, u32[]{:S(2)}, u32[]{:S(2)}) collective-permute-start(f32[4,1,64,128]{3,2,1,0:T(8,128)S(1)} %get-tuple-element.40), channel_id=1, source_target_pairs={{1,0},{2,1},{3,2},{5,4},{6,5},{7,6},{9,8},{10,9},{11,10},{13,12},{... | collective-permute-start | bytes 393224 | tf_op jit(solution)/shard_map/ppermute | solution.py:19
  28.3 4.8 %collective-permute-start.4 = (f32[4,1,64,128]{3,2,1,0:T(8,128)S(1)}, f32[4,1,64,128]{3,2,1,0:T(8,128)S(1)}, u32[]{:S(2)}, u32[]{:S(2)}) collective-permute-start(f32[4,1,64,128]{3,2,1,0:T(8,128)S(1)} %get-tuple-element.37), channel_id=1, source_target_pairs={{0,1},{1,2},{2,3},{4,5},{5,6},{6,7},{8,9},{9,10},{10,11},{12,13},{... | collective-permute-start | bytes 393224 | tf_op jit(solution)/shard_map/ppermute | solution.py:16
  31.2 5.7 %collective-permute-start.5 = (f32[4,1,64,128]{3,2,1,0:T(8,128)S(1)}, f32[4,1,64,128]{3,2,1,0:T(8,128)S(1)}, u32[]{:S(2)}, u32[]{:S(2)}) collective-permute-start(f32[4,1,64,128]{3,2,1,0:T(8,128)S(1)} %get-tuple-element.38), channel_id=1, source_target_pairs={{1,0},{2,1},{3,2},{5,4},{6,5},{7,6},{9,8},{10,9},{11,10},{13,12},{... | collective-permute-start | bytes 393224 | tf_op jit(solution)/shard_map/ppermute | solution.py:19
  39.6 5.7 %collective-permute-start.7 = (f32[4,1,64,128]{3,2,1,0:T(8,128)S(1)}, f32[4,1,64,128]{3,2,1,0:T(8,128)S(1)}, u32[]{:S(2)}, u32[]{:S(2)}) collective-permute-start(f32[4,1,64,128]{3,2,1,0:T(8,128)S(1)} %get-tuple-element.36), channel_id=1, source_target_pairs={{1,0},{2,1},{3,2},{5,4},{6,5},{7,6},{9,8},{10,9},{11,10},{13,12},{... | collective-permute-start | bytes 393224 | tf_op jit(solution)/shard_map/ppermute | solution.py:19
  47.6 5.7 %collective-permute-start.9 = (f32[4,1,64,128]{3,2,1,0:T(8,128)S(1)}, f32[4,1,64,128]{3,2,1,0:T(8,128)S(1)}, u32[]{:S(2)}, u32[]{:S(2)}) collective-permute-start(f32[4,1,64,128]{3,2,1,0:T(8,128)S(1)} %get-tuple-element.34), channel_id=1, source_target_pairs={{1,0},{2,1},{3,2},{5,4},{6,5},{7,6},{9,8},{10,9},{11,10},{13,12},{... | collective-permute-start | bytes 393224 | tf_op jit(solution)/shard_map/ppermute | solution.py:19
  55.7 5.7 %collective-permute-start.11 = (f32[4,1,64,128]{3,2,1,0:T(8,128)S(1)}, f32[4,1,64,128]{3,2,1,0:T(8,128)S(1)}, u32[]{:S(2)}, u32[]{:S(2)}) collective-permute-start(f32[4,1,64,128]{3,2,1,0:T(8,128)S(1)} %get-tuple-element.32), channel_id=1, source_target_pairs={{1,0},{2,1},{3,2},{5,4},{6,5},{7,6},{9,8},{10,9},{11,10},{13,12},{... | collective-permute-start | bytes 393224 | tf_op jit(solution)/shard_map/ppermute | solution.py:19
  63.9 6.3 %collective-permute-start.13 = (f32[4,1,64,128]{3,2,1,0:T(8,128)S(1)}, f32[4,1,64,128]{3,2,1,0:T(8,128)S(1)}, u32[]{:S(2)}, u32[]{:S(2)}) collective-permute-start(f32[4,1,64,128]{3,2,1,0:T(8,128)S(1)} %get-tuple-element.30), channel_id=1, source_target_pairs={{1,0},{2,1},{3,2},{5,4},{6,5},{7,6},{9,8},{10,9},{11,10},{13,12},{... | collective-permute-start | bytes 393224 | tf_op jit(solution)/shard_map/ppermute | solution.py:19
  72.3 7.0 %collective-permute-start.15 = (f32[4,1,64,128]{3,2,1,0:T(8,128)S(1)}, f32[4,1,64,128]{3,2,1,0:T(8,128)S(1)}, u32[]{:S(2)}, u32[]{:S(2)}) collective-permute-start(f32[4,1,64,128]{3,2,1,0:T(8,128)S(1)} %get-tuple-element.28), channel_id=1, source_target_pairs={{1,0},{2,1},{3,2},{5,4},{6,5},{7,6},{9,8},{10,9},{11,10},{13,12},{... | collective-permute-start | bytes 393224 | tf_op jit(solution)/shard_map/ppermute | solution.py:19
  81.9 6.1 %collective-permute-start.17 = (f32[4,1,64,128]{3,2,1,0:T(8,128)S(1)}, f32[4,1,64,128]{3,2,1,0:T(8,128)S(1)}, u32[]{:S(2)}, u32[]{:S(2)}) collective-permute-start(f32[4,1,64,128]{3,2,1,0:T(8,128)S(1)} %get-tuple-element.26), channel_id=1, source_target_pairs={{1,0},{2,1},{3,2},{5,4},{6,5},{7,6},{9,8},{10,9},{11,10},{13,12},{... | collective-permute-start | bytes 393224 | tf_op jit(solution)/shard_map/ppermute | solution.py:19
  90.7 5.7 %collective-permute-start.19 = (f32[4,1,64,128]{3,2,1,0:T(8,128)S(1)}, f32[4,1,64,128]{3,2,1,0:T(8,128)S(1)}, u32[]{:S(2)}, u32[]{:S(2)}) collective-permute-start(f32[4,1,64,128]{3,2,1,0:T(8,128)S(1)} %get-tuple-element.24), channel_id=1, source_target_pairs={{1,0},{2,1},{3,2},{5,4},{6,5},{7,6},{9,8},{10,9},{11,10},{13,12},{... | collective-permute-start | bytes 393224 | tf_op jit(solution)/shard_map/ppermute | solution.py:19
  99.1 5.7 %collective-permute-start.21 = (f32[4,1,64,128]{3,2,1,0:T(8,128)S(1)}, f32[4,1,64,128]{3,2,1,0:T(8,128)S(1)}, u32[]{:S(2)}, u32[]{:S(2)}) collective-permute-start(f32[4,1,64,128]{3,2,1,0:T(8,128)S(1)} %get-tuple-element.22), channel_id=1, source_target_pairs={{1,0},{2,1},{3,2},{5,4},{6,5},{7,6},{9,8},{10,9},{11,10},{13,12},{... | collective-permute-start | bytes 393224 | tf_op jit(solution)/shard_map/ppermute | solution.py:19
  107.5 5.7 %collective-permute-start.23 = (f32[4,1,64,128]{3,2,1,0:T(8,128)S(1)}, f32[4,1,64,128]{3,2,1,0:T(8,128)S(1)}, u32[]{:S(2)}, u32[]{:S(2)}) collective-permute-start(f32[4,1,64,128]{3,2,1,0:T(8,128)S(1)} %get-tuple-element.20), channel_id=1, source_target_pairs={{1,0},{2,1},{3,2},{5,4},{6,5},{7,6},{9,8},{10,9},{11,10},{13,12},{... | collective-permute-start | bytes 393224 | tf_op jit(solution)/shard_map/ppermute | solution.py:19
  115.6 5.7 %collective-permute-start.25 = (f32[4,1,64,128]{3,2,1,0:T(8,128)S(1)}, f32[4,1,64,128]{3,2,1,0:T(8,128)S(1)}, u32[]{:S(2)}, u32[]{:S(2)}) collective-permute-start(f32[4,1,64,128]{3,2,1,0:T(8,128)S(1)} %get-tuple-element.18), channel_id=1, source_target_pairs={{1,0},{2,1},{3,2},{5,4},{6,5},{7,6},{9,8},{10,9},{11,10},{13,12},{... | collective-permute-start | bytes 393224 | tf_op jit(solution)/shard_map/ppermute | solution.py:19
  123.8 5.7 %collective-permute-start.27 = (f32[4,1,64,128]{3,2,1,0:T(8,128)S(1)}, f32[4,1,64,128]{3,2,1,0:T(8,128)S(1)}, u32[]{:S(2)}, u32[]{:S(2)}) collective-permute-start(f32[4,1,64,128]{3,2,1,0:T(8,128)S(1)} %get-tuple-element.16), channel_id=1, source_target_pairs={{1,0},{2,1},{3,2},{5,4},{6,5},{7,6},{9,8},{10,9},{11,10},{13,12},{... | collective-permute-start | bytes 393224 | tf_op jit(solution)/shard_map/ppermute | solution.py:19
  131.9 5.8 %collective-permute-start.29 = (f32[4,1,64,128]{3,2,1,0:T(8,128)S(1)}, f32[4,1,64,128]{3,2,1,0:T(8,128)S(1)}, u32[]{:S(2)}, u32[]{:S(2)}) collective-permute-start(f32[4,1,64,128]{3,2,1,0:T(8,128)S(1)} %get-tuple-element.14), channel_id=1, source_target_pairs={{1,0},{2,1},{3,2},{5,4},{6,5},{7,6},{9,8},{10,9},{11,10},{13,12},{... | collective-permute-start | bytes 393224 | tf_op jit(solution)/shard_map/ppermute | solution.py:19
  139.1 34.0 %collective-permute-start.30 = (f32[2,4,1,64,128]{4,3,2,1,0:T(8,128)}, f32[2,4,1,64,128]{4,3,2,1,0:T(8,128)}, u32[]{:S(2)}, u32[]{:S(2)}) collective-permute-start(f32[2,4,1,64,128]{4,3,2,1,0:T(8,128)} %get-tuple-element.11), channel_id=1, source_target_pairs={{0,1},{1,2},{2,3},{4,5},{5,6},{6,7},{8,9},{9,10},{10,11},{12,13},{... | collective-permute-start | bytes 786440 | tf_op jit(solution)/shard_map/ppermute | solution.py:16
  141.7 31.4 %collective-permute-start.31 = (f32[2,4,1,64,128]{4,3,2,1,0:T(8,128)}, f32[2,4,1,64,128]{4,3,2,1,0:T(8,128)}, u32[]{:S(2)}, u32[]{:S(2)}) collective-permute-start(f32[2,4,1,64,128]{4,3,2,1,0:T(8,128)} %get-tuple-element.12), channel_id=1, source_target_pairs={{1,0},{2,1},{3,2},{5,4},{6,5},{7,6},{9,8},{10,9},{11,10},{13,12},{... | collective-permute-start | bytes 786440 | tf_op jit(solution)/shard_map/ppermute | solution.py:19
  144.2 46.2 %all-to-all-start = ((f32[4,64,512]{2,0,1:T(4,128)}), f32[4,64,512]{2,0,1:T(4,128)S(1)}, u32[]{:S(2)}, u32[]{:S(2)}) async-start(f32[4,64,512]{2,0,1:T(4,128)} %copy.7), calls=%async_computation | async-start | bytes 1048576 | tf_op jit(solution)/shard_map/all_to_all | solution.py:84
  190.4 23.6 %all-to-all-start.1 = ((f32[4,64,512]{2,0,1:T(4,128)}), f32[4,64,512]{2,0,1:T(4,128)S(1)}, u32[]{:S(2)}, u32[]{:S(2)}) async-start(f32[4,64,512]{2,0,1:T(4,128)} %copy.8), calls=%async_computation.1 | async-start | bytes 1048576 | tf_op jit(solution)/shard_map/all_to_all | solution.py:87
  196.7 191.1 %all-reduce.37.cloned.1.call-start = ((), (), s32[]{:S(2)}) async-start(), calls=%async_computation.3 | async-start | bytes 524288 | tf_op jit(solution)/shard_map/psum | solution.py:99
  215.6 216.6 %all-reduce.39.cloned.1.call-start = ((), (), s32[]{:S(2)}) async-start(), calls=%async_computation.4 | async-start | bytes 524288 | tf_op jit(solution)/shard_map/psum | solution.py:99
  (16 other events, 307.7 us)
Sparse Core Ops, SparseCore 0:
  215.7 172.0 all-reduce.36
  390.2 41.8 all-reduce.38
